TPU v7x, 32 devices: a whole 2x2x4 slice. The times are simulated.
32 devices in a mesh: dp: 8 (over z, x), tensor: 4 (over y, core).
Axes of the slice: x: 2, y: 2, z: 4, core: 2. Of those that a mesh axis runs over, the one named last changes fastest.
Arguments:
- inputs: bfloat16 [8, 64, 64, 1280], P('dp', 'tensor'), may hold values from -6 to 6
- cotangent: bfloat16 [8, 64, 64, 1280], P('dp', 'tensor'), may hold values from -6 to 6
- teacher: bfloat16 [8, 64, 64, 1280], P('dp', 'tensor'), may hold values from -6 to 6
- qkv_weight: bfloat16 [3, 1280, 1280], P(None, 'dp', 'tensor'), may hold values from -0.15625 to 0.15625
- proj_weight: bfloat16 [1280, 1280], P('tensor', 'dp'), may hold values from -1 to 1
- up_weight: bfloat16 [1280, 5120], P('dp', 'tensor'), may hold values from -0.15625 to 0.15625
- down_weight: bfloat16 [5120, 1280], P('tensor', 'dp'), may hold values from -0.078125 to 0.078125
- qv_bias: bfloat16 [2, 1280], P(None, 'tensor'), may hold values from -3 to 3
- up_bias: bfloat16 [5120], P('tensor'), may hold values from -3 to 3
- norm_gains: bfloat16 [2, 1280], replicated, may hold values from 0.5 to 1.5
- norm_shifts: bfloat16 [2, 1280], replicated, may hold values from -3 to 3
- out_biases: bfloat16 [2, 1280], replicated, may hold values from -3 to 3
- rel_tables: bfloat16 [2, 27, 80], replicated, may hold values from -0.625 to 0.625
Outputs:
- output: bfloat16 [8, 64, 64, 1280], P('dp', 'tensor')
- input_grad: float32 [8, 64, 64, 1280], P('dp', 'tensor')
- loss: float32 [], replicated
- qkv_weight_grad: float32 [3, 1280, 1280], P(None, 'dp', 'tensor')
- proj_weight_grad: float32 [1280, 1280], P('tensor', 'dp')
- up_weight_grad: float32 [1280, 5120], P('dp', 'tensor')
- down_weight_grad: float32 [5120, 1280], P('tensor', 'dp')
- qv_bias_grad: float32 [2, 1280], P(None, 'tensor')
- up_bias_grad: float32 [5120], P('tensor')
- norm_gains_grad: float32 [2, 1280], replicated
- norm_shifts_grad: float32 [2, 1280], replicated
- out_biases_grad: float32 [2, 1280], replicated
- rel_tables_grad: float32 [2, 27, 80], replicated
All inputs are finite; a program needn't handle non-finite values.
Results may differ from a plain program's by a relative error of at most 0.013.
Values may be sent and summed in bfloat16 or wider, within the bound.
A program may use at most 256 MiB of HBM per device.

v0:
```python
from functools import partial
import jax
import jax.numpy as jnp
from jax import lax
from jax.sharding import PartitionSpec as P

D = 1280
HEAD_DIM = 80
GRID = 64
WIN = 14
PGRID = 70
NWIN = 5
highest = lax.Precision.HIGHEST


def layer_norm(values, gain_vector, shift_vector):
    average = jnp.mean(values, axis=-1, keepdims=True)
    centred = values - average
    variance = jnp.mean(centred * centred, axis=-1, keepdims=True)
    return centred * lax.rsqrt(variance + 1e-06) * gain_vector + shift_vector


def exact_gelu(values):
    return jax.nn.gelu(values, approximate=False)


def offset_tables(window):
    position = jnp.arange(window * window)
    across = jnp.arange(window)
    ranks = jnp.arange(2 * window - 1)
    high_sel = (
        position[:, None, None] // window - across[None, :, None] + window - 1
        == ranks[None, None, :]
    ).astype(jnp.float32)
    wide_sel = (
        position[:, None, None] % window - across[None, :, None] + window - 1
        == ranks[None, None, :]
    ).astype(jnp.float32)
    return (high_sel, wide_sel)


def to_windows(grid_values):
    extra = PGRID - GRID
    padded = jnp.pad(grid_values, ((0, extra), (0, extra), (0, 0)))
    channels = grid_values.shape[-1]
    shaped = padded.reshape(NWIN, WIN, NWIN, WIN, channels).transpose(0, 2, 1, 3, 4)
    return shaped.reshape(NWIN, NWIN, WIN * WIN, channels)


def from_windows(windowed):
    channels = windowed.shape[-1]
    shaped = windowed.reshape(NWIN, NWIN, WIN, WIN, channels).transpose(0, 2, 1, 3, 4)
    return shaped.reshape(PGRID, PGRID, channels)[:GRID, :GRID]


def score_block(queries, key_rows, tables, selectors):
    table_high, table_wide = tables
    high_sel, wide_sel = selectors
    raw = jnp.einsum(
        "wqhc,wkhc->whqk", queries, key_rows, preferred_element_type=jnp.float32
    ) * HEAD_DIM ** (-0.5)
    along_high = jnp.einsum(
        "wqhc,rc->wqhr", queries, table_high, preferred_element_type=jnp.float32
    )
    along_wide = jnp.einsum(
        "wqhc,rc->wqhr", queries, table_wide, preferred_element_type=jnp.float32
    )
    bias_high = jnp.einsum("wqhr,qkr->whqk", along_high, high_sel, precision=highest)
    bias_wide = jnp.einsum("wqhr,qkr->whqk", along_wide, wide_sel, precision=highest)
    shaped = (
        raw.reshape(raw.shape[:3] + (WIN, WIN)) + bias_high[..., :, None] + bias_wide[..., None, :]
    )
    return shaped.reshape(raw.shape)


def attend_row(block_parts, tables, selectors):
    queries, key_rows, value_rows = block_parts
    scores = score_block(queries, key_rows, tables, selectors)
    row_max = jnp.max(scores, axis=-1, keepdims=True)
    shifted = jnp.exp(scores - row_max)
    row_total = jnp.sum(shifted, axis=-1, keepdims=True)
    probs_low = (shifted / row_total).astype(jnp.bfloat16)
    attended = jnp.einsum(
        "whqk,wkhc->wqhc", probs_low, value_rows, preferred_element_type=jnp.float32
    )
    return (attended.astype(jnp.bfloat16), (row_max + jnp.log(row_total))[..., 0])


def attend_back(block_parts, tables, selectors):
    queries, key_rows, value_rows, attended_grad, log_total = block_parts
    high_sel, wide_sel = selectors
    scores = score_block(queries, key_rows, tables, selectors)
    probs = jnp.exp(scores - log_total[..., None])
    probs_grad = jnp.einsum(
        "wqhc,wkhc->whqk", attended_grad, value_rows, preferred_element_type=jnp.float32
    )
    value_grad = jnp.einsum(
        "whqk,wqhc->wkhc",
        probs.astype(jnp.bfloat16),
        attended_grad,
        preferred_element_type=jnp.float32,
    )
    scores_grad = probs * (probs_grad - jnp.sum(probs * probs_grad, axis=-1, keepdims=True))
    scores_low = scores_grad.astype(jnp.bfloat16)
    query_grad = jnp.einsum(
        "whqk,wkhc->wqhc", scores_low, key_rows, preferred_element_type=jnp.float32
    ) * HEAD_DIM ** (-0.5)
    key_grad = jnp.einsum(
        "whqk,wqhc->wkhc", scores_low, queries, preferred_element_type=jnp.float32
    ) * HEAD_DIM ** (-0.5)
    shaped = scores_grad.reshape(scores_grad.shape[:3] + (WIN, WIN))
    rank_high = jnp.einsum("whqa,qar->wqhr", jnp.sum(shaped, axis=-1), high_sel, precision=highest)
    rank_wide = jnp.einsum("whqb,qbr->wqhr", jnp.sum(shaped, axis=-2), wide_sel, precision=highest)
    table_high = tables[0].astype(jnp.float32)
    table_wide = tables[1].astype(jnp.float32)
    query_grad = query_grad + jnp.einsum("wqhr,rc->wqhc", rank_high, table_high, precision=highest)
    query_grad = query_grad + jnp.einsum("wqhr,rc->wqhc", rank_wide, table_wide, precision=highest)
    query_wide = queries.astype(jnp.float32)
    table_grad = jnp.stack(
        [
            jnp.einsum("wqhr,wqhc->rc", rank_high, query_wide, precision=highest),
            jnp.einsum("wqhr,wqhc->rc", rank_wide, query_wide, precision=highest),
        ]
    )
    return (query_grad, key_grad, value_grad, table_grad)


def shards(
    inputs,
    cotangent,
    teacher,
    qkv_weight,
    proj_weight,
    up_weight,
    down_weight,
    qv_bias,
    up_bias,
    norm_gains,
    norm_shifts,
    out_biases,
    rel_tables,
):
    qkv_full, proj_full, up_full, down_full = (
        lax.all_gather(qkv_weight, "dp", axis=1, tiled=True),
        lax.all_gather(proj_weight, "dp", axis=1, tiled=True),
        lax.all_gather(up_weight, "dp", axis=0, tiled=True),
        lax.all_gather(down_weight, "dp", axis=1, tiled=True),
    )
    up_matrix, down_matrix, up_bias_all = (up_full, down_full, up_bias)
    images, row_count = (inputs.shape[0], inputs.shape[1])
    local_width = qkv_full.shape[2]
    head_count = local_width // HEAD_DIM
    head_shape = (NWIN, NWIN, WIN * WIN, head_count, HEAD_DIM)
    selectors = offset_tables(WIN)
    tables = (rel_tables[0], rel_tables[1])
    gains_wide = norm_gains.astype(jnp.float32)
    shifts_wide = norm_shifts.astype(jnp.float32)
    source = inputs[0].astype(jnp.float32)
    normed = layer_norm(source, gains_wide[0], shifts_wide[0]).astype(jnp.bfloat16)
    gathered = lax.all_gather(normed, "tensor", axis=0, tiled=True)
    windows = to_windows(gathered)
    projected = jnp.einsum("abpd,sdc->sabpc", windows, qkv_full, preferred_element_type=jnp.float32)
    queries = (projected[0] + qv_bias[0]).astype(jnp.bfloat16).reshape(head_shape)
    key_rows = projected[1].astype(jnp.bfloat16).reshape(head_shape)
    value_rows = (projected[2] + qv_bias[1]).astype(jnp.bfloat16).reshape(head_shape)
    attended, log_totals = lax.map(
        partial(attend_row, tables=tables, selectors=selectors), (queries, key_rows, value_rows)
    )
    grid_out = from_windows(attended.reshape(NWIN, NWIN, WIN * WIN, local_width))
    row_piece = grid_out
    attn_branch = lax.psum_scatter(
        jnp.einsum("xyc,cd->xyd", row_piece, proj_full, preferred_element_type=jnp.float32).astype(
            jnp.bfloat16
        ),
        "tensor",
        scatter_dimension=0,
        tiled=True,
    ).astype(jnp.float32)
    middle = source + attn_branch + out_biases[0].astype(jnp.float32)
    normed_two = layer_norm(middle, gains_wide[1], shifts_wide[1]).astype(jnp.bfloat16)
    mlp_input = lax.all_gather(normed_two, "tensor", axis=0, tiled=True)
    hidden = (
        jnp.einsum("xyd,dm->xym", mlp_input, up_matrix, preferred_element_type=jnp.float32)
        + up_bias_all
    )
    active = exact_gelu(hidden).astype(jnp.bfloat16)
    row_piece = active
    mlp_branch = lax.psum_scatter(
        jnp.einsum(
            "xym,md->xyd", row_piece, down_matrix, preferred_element_type=jnp.float32
        ).astype(jnp.bfloat16),
        "tensor",
        scatter_dimension=0,
        tiled=True,
    ).astype(jnp.float32)
    result = middle + mlp_branch + out_biases[1].astype(jnp.float32)
    mismatch = result - teacher[0].astype(jnp.float32)
    loss_total = jnp.sum(mismatch * mismatch)
    outputs = [result.astype(jnp.bfloat16)]
    result_grad = cotangent[0].astype(jnp.float32) + mismatch
    result_low = result_grad.astype(jnp.bfloat16)
    grad_rows = lax.all_gather(result_low, "tensor", axis=0, tiled=True)
    down_acc = jnp.einsum("xym,xyd->md", active, grad_rows, preferred_element_type=jnp.float32)
    active_grad = jnp.einsum(
        "xyd,md->xym", grad_rows, down_matrix, preferred_element_type=jnp.float32
    )
    gelu_value, gelu_back = jax.vjp(exact_gelu, hidden)
    hidden_grad = gelu_back(active_grad)[0]
    up_bias_acc = jnp.sum(hidden_grad, axis=(0, 1))
    hidden_low = hidden_grad.astype(jnp.bfloat16)
    up_acc = jnp.einsum("xyd,xym->dm", mlp_input, hidden_low, preferred_element_type=jnp.float32)
    row_piece = hidden_low
    second_grad = lax.psum_scatter(
        jnp.einsum("xym,dm->xyd", row_piece, up_matrix, preferred_element_type=jnp.float32).astype(
            jnp.bfloat16
        ),
        "tensor",
        scatter_dimension=0,
        tiled=True,
    ).astype(jnp.float32)
    second_value, second_back = jax.vjp(layer_norm, middle, gains_wide[1], shifts_wide[1])
    middle_part, second_gain, second_shift = second_back(second_grad)
    middle_grad = result_grad + middle_part
    out_bias_acc = jnp.stack([jnp.sum(middle_grad, axis=(0, 1)), jnp.sum(result_grad, axis=(0, 1))])
    middle_low = middle_grad.astype(jnp.bfloat16)
    gathered_grad = lax.all_gather(middle_low, "tensor", axis=0, tiled=True)
    proj_acc = jnp.einsum(
        "xyc,xyd->cd", grid_out, gathered_grad, preferred_element_type=jnp.float32
    )
    attended_grad = jnp.einsum(
        "xyd,cd->xyc", gathered_grad, proj_full, preferred_element_type=jnp.float32
    ).astype(jnp.bfloat16)
    grad_windows = to_windows(attended_grad).reshape(head_shape)
    query_grad, key_grad, value_grad, table_parts = lax.map(
        partial(attend_back, tables=tables, selectors=selectors),
        (queries, key_rows, value_rows, grad_windows, log_totals),
    )
    table_acc = jnp.sum(table_parts, axis=0)
    query_flat = query_grad.reshape(NWIN, NWIN, WIN * WIN, local_width)
    key_flat = key_grad.reshape(NWIN, NWIN, WIN * WIN, local_width)
    value_flat = value_grad.reshape(NWIN, NWIN, WIN * WIN, local_width)
    qv_acc = jnp.stack([jnp.sum(query_flat, axis=(0, 1, 2)), jnp.sum(value_flat, axis=(0, 1, 2))])
    stacked = jnp.stack([query_flat, key_flat, value_flat]).astype(jnp.bfloat16)
    qkv_acc = jnp.einsum("abpd,sabpc->sdc", windows, stacked, preferred_element_type=jnp.float32)
    normed_back = jnp.einsum(
        "sabpc,sdc->abpd", stacked, qkv_full, preferred_element_type=jnp.float32
    )
    first_grad = lax.psum_scatter(
        from_windows(normed_back).astype(jnp.bfloat16), "tensor", scatter_dimension=0, tiled=True
    ).astype(jnp.float32)
    first_value, first_back = jax.vjp(layer_norm, source, gains_wide[0], shifts_wide[0])
    source_part, first_gain, first_shift = first_back(first_grad)
    gain_acc = jnp.stack([first_gain, second_gain])
    shift_acc = jnp.stack([first_shift, second_shift])
    input_grads = [middle_grad + source_part]
    qkv_grad, proj_grad, up_grad, down_grad = (
        lax.psum_scatter(
            qkv_acc.astype(jnp.bfloat16), "dp", scatter_dimension=1, tiled=True
        ).astype(jnp.float32),
        lax.psum_scatter(
            proj_acc.astype(jnp.bfloat16), "dp", scatter_dimension=1, tiled=True
        ).astype(jnp.float32),
        lax.psum_scatter(up_acc.astype(jnp.bfloat16), "dp", scatter_dimension=0, tiled=True).astype(
            jnp.float32
        ),
        lax.psum_scatter(
            down_acc.astype(jnp.bfloat16), "dp", scatter_dimension=1, tiled=True
        ).astype(jnp.float32),
    )
    qv_grad, up_bias_grad = lax.psum((qv_acc, up_bias_acc), "dp")
    gains_grad, shifts_grad, out_grad, table_grad, loss_sum = lax.psum(
        (gain_acc, shift_acc, out_bias_acc, table_acc, loss_total), ("dp", "tensor")
    )
    element_count = images * row_count * GRID * D * lax.axis_size("dp") * lax.axis_size("tensor")
    loss = loss_sum / element_count
    return (
        jnp.stack(outputs),
        jnp.stack(input_grads),
        loss,
        qkv_grad,
        proj_grad,
        up_grad,
        down_grad,
        qv_grad,
        up_bias_grad,
        gains_grad,
        shifts_grad,
        out_grad,
        table_grad,
    )


def solution(mesh):
    in_specs = (
        P("dp", "tensor", None, None),
        P("dp", "tensor", None, None),
        P("dp", "tensor", None, None),
        P(None, "dp", "tensor"),
        P("tensor", "dp"),
        P("dp", "tensor"),
        P("tensor", "dp"),
        P(None, "tensor"),
        P("tensor"),
        P(),
        P(),
        P(),
        P(),
    )
    out_specs = (
        P("dp", "tensor", None, None),
        P("dp", "tensor", None, None),
        P(),
        P(None, "dp", "tensor"),
        P("tensor", "dp"),
        P("dp", "tensor"),
        P("tensor", "dp"),
        P(None, "tensor"),
        P("tensor"),
        P(),
        P(),
        P(),
        P(),
    )
    return jax.shard_map(shards, mesh=mesh, in_specs=in_specs, out_specs=out_specs, check_vma=False)
```

profile of v0, /device:TPU:0, one launch (start us, length us, event | category | flops | bytes accessed | tf_op | source)
XLA Modules:
  0.0 2018.4 jit_solution(13288147670114072156)
XLA Ops:
  18.5 36.7 %all_gather.26 = bf16[320,1280]{0,1:T(8,128)(2,1)} all-gather(bf16[320,160]{0,1:T(8,128)(2,1)S(1)} %copy-done.44), channel_id=1, replica_groups=mesh['dp'=8,'tensor'=4] {'dp'}, dimensions={1}, use_global_device_ids=true | all-gather | bytes 921600 | tf_op jit(solution)/shard_map/all_gather | solution.py:145
  55.2 34.5 %all-gather.8.cloned.1.call-done = bf16[64,64,1280]{2,1,0:T(8,128)(2,1)} async-done(((bf16[16,64,1280]{2,1,0:T(8,128)(2,1)}), bf16[64,64,1280]{2,1,0:T(8,128)(2,1)}) %all-gather.8.cloned.1.call-update) | async-done | bytes 10485776 | tf_op jit(solution)/shard_map/all_gather | solution.py:160
  99.9 18.6 reshape.295
  118.5 13.4 copy.189
  131.9 19.4 reshape.319
  151.3 24.5 %fusion.109 = f32[3,5,5,196,320]{4,3,0,2,1:T(8,128)} fusion(bf16[5,5,196,1280,1]{3,2,1,0,4:T(8,128)(2,1)} %reshape.319, bf16[3,1280,320]{2,1,0:T(8,128)(2,1)} %all-gather.10.cloned.1.call-done), kind=kOutput, calls=%fused_computation.142 | convolution fusion | flops 12042240000 | bytes 33817600 | tf_op jit(solution)/shard_map/abpd,sdc->sabpc/dot_general | solution.py:162
  175.8 11.8 fusion.165
  231.1 193.3 %while.31 = (s32[]{:T(128)}, bf16[5,5,196,4,80]{2,4,3,1,0:T(8,128)(2,1)}, f32[5,5,4,196]{3,2,1,0:T(4,128)}, bf16[5,5,196,4,80]{2,4,3,1,0:T(8,128)(2,1)}, bf16[5,...) while((s32[]{:T(128)}, ...), condition=%wide.region_5.6_spmd.clone, body=%wide.region_2.5_spmd.clone.sunk | while | flops 322814336 | bytes 44160668 | solution.py:166
  424.5 11.4 copy.121
  470.1 84.2 %reduce-scatter.11.cloned.1.call-done = bf16[16,64,1280]{2,1,0:T(8,128)(2,1)} async-done(((bf16[64,64,1280]{2,1,0:T(8,128)(2,1)}), bf16[16,64,1280]{2,1,0:T(8,128)(2,1)}) %reduce-scatter.11.cloned.1.call-update) | async-done | bytes 2621456 | tf_op jit(solution)/shard_map/reduce_scatter | solution.py:171
  562.9 55.4 %all-gather.14.cloned.1.call-done = bf16[1280,1280]{1,0:T(8,128)(2,1)} async-done(((bf16[160,1280]{1,0:T(8,128)(2,1)}), bf16[1280,1280]{1,0:T(8,128)(2,1)}) %all-gather.14.cloned.1.call-update) | async-done | bytes 3276816 | tf_op jit(solution)/shard_map/all_gather | solution.py:146
  618.3 70.8 %all-gather.12.cloned.1.call-done = bf16[64,64,1280]{2,1,0:T(8,128)(2,1)} async-done(((bf16[16,64,1280]{2,1,0:T(8,128)(2,1)}), bf16[64,64,1280]{2,1,0:T(8,128)(2,1)}) %all-gather.12.cloned.1.call-update) | async-done | bytes 10485776 | tf_op jit(solution)/shard_map/all_gather | solution.py:181
  689.1 60.9 %multiply_convert_fusion = (bf16[64,64,1280]{2,1,0:T(8,128)(2,1)}, f32[64,64,1280]{2,1,0:T(8,128)}, f32[64,64,1280]{2,1,0:T(8,128)}) fusion(f32[1280]{0:T(1024)S(1)} %convert_element_type.209, bf16[64,64,1280]{2,1,0:T(8,128)(2,1)} %all-gather.12.cloned.1.call-done, bf16[1280,1280]{1,0:T(8,128)(2,1)} %all-gather.14.cloned.1.call-done), kind=kOutput, calls=%fused_computation.117 | convolution fusion | flops 13767802880 | bytes 66196480 | tf_op jit(solution)/shard_map/xyd,dm->xym/dot_general | solution.py:183
  753.2 20.1 convolution_convert_fusion.1
  773.4 84.0 %reduce-scatter.13.cloned.1.call-done = bf16[16,64,1280]{2,1,0:T(8,128)(2,1)} async-done(((bf16[64,64,1280]{2,1,0:T(8,128)(2,1)}), bf16[16,64,1280]{2,1,0:T(8,128)(2,1)}) %reduce-scatter.13.cloned.1.call-update) | async-done | bytes 2621456 | tf_op jit(solution)/shard_map/reduce_scatter | solution.py:188
  868.4 70.3 %all-gather.18.cloned.1.call-done = bf16[64,64,1280]{2,1,0:T(8,128)(2,1)} async-done(((bf16[16,64,1280]{2,1,0:T(8,128)(2,1)}), bf16[64,64,1280]{2,1,0:T(8,128)(2,1)}) %all-gather.18.cloned.1.call-update) | async-done | bytes 10485776 | tf_op jit(solution)/shard_map/all_gather | solution.py:202
  938.7 30.7 %fusion.169 = (f32[1280]{0:T(1024)}, bf16[64,64,1280]{2,1,0:T(8,128)(2,1)}) fusion(f32[64,64,1280]{2,1,0:T(8,128)} %get-tuple-element.416, f32[64,64,1280]{2,1,0:T(8,128)} %get-tuple-element.430, bf16[64,64,1280]{2,1,0:T(8,128)(2,1)} %all-gather.18.cloned.1.call-done, bf16[1280,1280]{0,1:T(8,128)(2,1)} %all-gather.16.cloned.1.call-done), kind=kOutput, calls=%fused_computation.252 | convolution fusion | flops 13500414976 | bytes 66196480 | tf_op jit(solution)/shard_map/xyd,md->xym/dot_general | solution.py:204
  969.4 19.9 convolution_convert_fusion
  989.4 85.4 %reduce-scatter.15.cloned.1.call-done = bf16[16,64,1280]{2,1,0:T(8,128)(2,1)} async-done(((bf16[64,64,1280]{2,1,0:T(8,128)(2,1)}), bf16[16,64,1280]{2,1,0:T(8,128)(2,1)}) %reduce-scatter.15.cloned.1.call-update) | async-done | bytes 2621456 | tf_op jit(solution)/shard_map/reduce_scatter | solution.py:213
  1096.3 20.8 %fusion.112 = bf16[1280,1280]{0,1:T(8,128)(2,1)} fusion(bf16[64,64,1280]{2,1,0:T(8,128)(2,1)} %get-tuple-element.415, bf16[64,64,1280]{2,1,0:T(8,128)(2,1)} %all-gather.18.cloned.1.call-done), kind=kOutput, calls=%fused_computation.156 | convolution fusion | flops 13423411200 | bytes 24248320 | tf_op jit(solution)/shard_map/xym,xyd->md/dot_general | solution.py:203
  1117.2 21.1 %fusion.113 = bf16[1280,1280]{1,0:T(8,128)(2,1)} fusion(bf16[64,64,1280]{2,1,0:T(8,128)(2,1)} %all-gather.12.cloned.1.call-done, bf16[64,64,1280]{2,1,0:T(8,128)(2,1)} %get-tuple-element.432), kind=kOutput, calls=%fused_computation.157 | convolution fusion | flops 13423411200 | bytes 24248320 | tf_op jit(solution)/shard_map/xyd,xym->dm/dot_general | solution.py:211
  1138.4 28.2 %all-gather.20.cloned.1.call-done = bf16[64,64,1280]{2,1,0:T(8,128)(2,1)} async-done(((bf16[16,64,1280]{2,1,0:T(8,128)(2,1)}), bf16[64,64,1280]{2,1,0:T(8,128)(2,1)}) %all-gather.20.cloned.1.call-update) | async-done | bytes 10485776 | tf_op jit(solution)/shard_map/all_gather | solution.py:226
  1199.8 11.4 copy.124
  1211.2 468.2 %while.32 = (s32[]{:T(128)}, f32[5,5,196,4,80]{2,4,3,1,0:T(8,128)}, bf16[5,5,196,4,80]{2,4,3,1,0:T(8,128)(2,1)}, f32[5,5,196,4,80]{2,4,3,1,0:T(8,128)}, f32[5,2,...) while((s32[]{:T(128)}, f32[5,5,196,4,80]{2,4,3,1,0:T(8,128)}, ...), condition=%wide.region_17.18_spmd.clone.clone, body=%wide.region_13.17_spmd.clone.clone.sunk | while | flops 1137800704 | bytes 142737584 | solution.py:234
  1731.4 17.5 fusion.143
  1763.5 25.8 %bitcast_convert_fusion = bf16[5,5,196,1280]{3,2,1,0:T(8,128)(2,1)} fusion(bf16[1,5,5,196,320]{4,3,0,2,1:T(8,128)(2,1)} %copy.127, bf16[1,5,5,196,320]{4,3,0,2,1:T(8,128)(2,1)} %copy.126, bf16[1,5,5,196,320]{4,3,0,2,1:T(8,128)(2,1)} %copy.125, bf16[3,1280,320]{2,1,0:T(8,128)(2,1)} %all-gather.10.cloned.1.call-done), kind=kOutput, calls=%fused_computation.114 | convolution fusion | flops 12057920512 | bytes 24409600 | tf_op jit(solution)/shard_map/sabpc,sdc->abpd/dot_general | solution.py:245
  1789.3 19.4 reshape.299
  1808.7 13.0 copy.188
  1821.7 18.7 reshape.300
  1854.8 37.5 %all-reduce.3 = (f32[2,320]{1,0:T(2,128)}, f32[1280]{0:T(1024)}) all-reduce(f32[2,320]{1,0:T(2,128)S(1)} %pad_maximum_fusion.10, f32[1280]{0:T(1024)S(1)} %copy-done.57), channel_id=1, replica_groups=mesh['dp'=8,'tensor'=4] {'dp'}, use_global_device_ids=true, to_apply=%region_29.30 | all-reduce | flops 1920 | bytes 15360 | tf_op jit(solution)/shard_map/psum | solution.py:270
  1898.7 56.9 %reduce-scatter.17.cloned.1.call-done = bf16[16,64,1280]{2,1,0:T(8,128)(2,1)} async-done(((bf16[64,64,1280]{2,1,0:T(8,128)(2,1)}), bf16[16,64,1280]{2,1,0:T(8,128)(2,1)}) %reduce-scatter.17.cloned.1.call-update) | async-done | bytes 2621456 | tf_op jit(solution)/shard_map/reduce_scatter | solution.py:248
  1962.5 41.0 %all-reduce.2 = (f32[]{:T(128)}, f32[2,1280]{1,0:T(2,128)}, f32[2,1280]{1,0:T(2,128)}, f32[2,1280]{1,0:T(2,128)}, f32[2,27,80]{2,1,0:T(8,128)S(1)}) all-reduce(f32[]{:T(128)} %get-tuple-element.343, f32[2,1280]{1,0:T(2,128)S(1)} %pad_maximum_fusion.7, ...), channel_id=1, replica_groups=mesh['dp'=8,'tensor'=4] {'dp','tensor'}, use_global_device_ids=true, to_apply=%region_22.23 | all-reduce | flops 12001 | bytes 96008 | tf_op jit(solution)/shard_map/psum | solution.py:271
  (555 shorter events, 928.3 us)
Async XLA Ops:
  7.2 82.5 %all-gather.8.cloned.1.call-start = ((), (), s32[]{:S(2)}) async-start(), calls=%async_computation.8 | async-start | bytes 13107200 | tf_op jit(solution)/shard_map/all_gather | solution.py:160
  16.7 134.6 %all-gather.10.cloned.1.call-start = ((), (), s32[]{:S(2)}) async-start(), calls=%async_computation.9 | async-start | bytes 3317760 | tf_op jit(solution)/shard_map/all_gather | solution.py:144
  17.4 536.9 %reduce-scatter.11.cloned.1.call-start = ((), (), s32[]{:S(2)}) async-start(), calls=%async_computation.10 | async-start | bytes 13107200 | tf_op jit(solution)/shard_map/reduce_scatter | solution.py:171
  424.5 21.5 %copy-start.18 = (s32[196,14]{1,0:T(8,128)}, s32[196,14]{1,0:T(8,128)S(1)}, u32[]{:S(2)}) copy-start(s32[196,14]{1,0:T(8,128)S(1)} %get-tuple-element.697) | copy-start | bytes 32932
  424.5 21.5 %copy-start.24 = (bf16[27,80]{1,0:T(8,128)(2,1)}, bf16[27,80]{1,0:T(8,128)(2,1)S(1)}, u32[]{:S(2)}) copy-start(bf16[27,80]{1,0:T(8,128)(2,1)S(1)} %get-tuple-element.724) | copy-start | bytes 12964
  468.8 85.6 %copy-start.5 = (bf16[1,16,64,1280]{3,2,1,0:T(8,128)(2,1)S(1)}, bf16[1,16,64,1280]{3,2,1,0:T(8,128)(2,1)}, u32[]{:S(2)}) copy-start(bf16[1,16,64,1280]{3,2,1,0:T(8,128)(2,1)} %param.17) | copy-start | bytes 7864324
  468.8 149.6 %all-gather.14.cloned.1.call-start = ((), (), s32[]{:S(2)}) async-start(), calls=%async_computation.12 | async-start | bytes 3686400 | tf_op jit(solution)/shard_map/all_gather | solution.py:146
  469.4 219.8 %all-gather.12.cloned.1.call-start = ((), (), s32[]{:S(2)}) async-start(), calls=%async_computation.11 | async-start | bytes 13107200 | tf_op jit(solution)/shard_map/all_gather | solution.py:181
  470.1 89.0 %copy-start.30 = (f32[1280]{0:T(1024)}, f32[1280]{0:T(1024)S(1)}, u32[]{:S(2)}) copy-start(f32[1280]{0:T(1024)S(1)} %get-tuple-element.352) | copy-start | bytes 15364
  562.3 190.9 %all-gather.16.cloned.1.call-start = ((), (), s32[]{:S(2)}) async-start(), calls=%async_computation.13 | async-start | bytes 3686400 | tf_op jit(solution)/shard_map/all_gather | solution.py:147
  562.9 294.5 %reduce-scatter.13.cloned.1.call-start = ((), (), s32[]{:S(2)}) async-start(), calls=%async_computation.14 | async-start | bytes 13107200 | tf_op jit(solution)/shard_map/reduce_scatter | solution.py:188
  773.3 84.1 %copy-start.6 = (bf16[1,16,64,1280]{3,2,1,0:T(8,128)(2,1)S(1)}, bf16[1,16,64,1280]{3,2,1,0:T(8,128)(2,1)}, u32[]{:S(2)}) copy-start(bf16[1,16,64,1280]{3,2,1,0:T(8,128)(2,1)} %param.17) | copy-start | bytes 7864324
  773.3 84.1 %copy-start.31 = (f32[1280]{0:T(1024)S(1)}, f32[1280]{0:T(1024)}, u32[]{:S(2)}) copy-start(f32[1280]{0:T(1024)} %copy-done.30) | copy-start | bytes 15364
  773.3 84.1 %copy-start.45 = (f32[1280]{0:T(1024)S(1)}, f32[1280]{0:T(1024)}, u32[]{:S(2)}) copy-start(f32[1280]{0:T(1024)} %get-tuple-element.353) | copy-start | bytes 15364
  773.3 165.4 %all-gather.18.cloned.1.call-start = ((), (), s32[]{:S(2)}) async-start(), calls=%async_computation.15 | async-start | bytes 13107200 | tf_op jit(solution)/shard_map/all_gather | solution.py:202
  868.3 206.5 %reduce-scatter.15.cloned.1.call-start = ((), (), s32[]{:S(2)}) async-start(), calls=%async_computation.16 | async-start | bytes 13107200 | tf_op jit(solution)/shard_map/reduce_scatter | solution.py:213
  989.3 85.5 %copy-start.35 = (f32[16,64]{1,0:T(8,128)S(1)}, f32[16,64]{1,0:T(8,128)}, u32[]{:S(2)}) copy-start(f32[16,64]{1,0:T(8,128)} %copy-done.34) | copy-start | bytes 12292
  989.3 85.5 %copy-start.39 = (f32[1280]{0:T(1024)S(1)}, f32[1280]{0:T(1024)}, u32[]{:S(2)}) copy-start(f32[1280]{0:T(1024)} %get-tuple-element.349) | copy-start | bytes 15364
  989.3 90.7 %copy-start.49 = (f32[16,64]{1,0:T(8,128)S(1)}, f32[16,64]{1,0:T(8,128)}, u32[]{:S(2)}) copy-start(f32[16,64]{1,0:T(8,128)} %copy-done.48) | copy-start | bytes 12292
  989.4 90.7 %copy-start.43 = (f32[16,64]{1,0:T(8,128)S(1)}, f32[16,64]{1,0:T(8,128)}, u32[]{:S(2)}) copy-start(f32[16,64]{1,0:T(8,128)} %copy-done.42) | copy-start | bytes 12292
  989.4 177.2 %all-gather.20.cloned.1.call-start = ((), (), s32[]{:S(2)}) async-start(), calls=%async_computation.17 | async-start | bytes 13107200 | tf_op jit(solution)/shard_map/all_gather | solution.py:226
  1096.2 754.0 %reduce-scatter.23.cloned.1.call-start = ((), (), s32[]{:S(2)}) async-start(), calls=%async_computation.21 | async-start | bytes 3686400 | tf_op jit(solution)/shard_map/reduce_scatter | solution.py:266
  1117.1 735.3 %reduce-scatter.21.cloned.1.call-start = ((), (), s32[]{:S(2)}) async-start(), calls=%async_computation.20 | async-start | bytes 3686400 | tf_op jit(solution)/shard_map/reduce_scatter | solution.py:263
  1117.2 49.4 %copy-start.29 = (bf16[320,1280]{0,1:T(8,128)(2,1)S(1)}, bf16[320,1280]{0,1:T(8,128)(2,1)}, u32[]{:S(2)}) copy-start(bf16[320,1280]{0,1:T(8,128)(2,1)} %all_gather.26) | copy-start | bytes 2457604
  1138.4 753.9 %reduce-scatter.19.cloned.1.call-start = ((), (), s32[]{:S(2)}) async-start(), calls=%async_computation.19 | async-start | bytes 1105920 | tf_op jit(solution)/shard_map/reduce_scatter | solution.py:260
  1731.3 162.5 %reduce-scatter.25.cloned.1.call-start = ((), (), s32[]{:S(2)}) async-start(), calls=%async_computation.22 | async-start | bytes 2949120
  1763.4 192.2 %reduce-scatter.17.cloned.1.call-start = ((), (), s32[]{:S(2)}) async-start(), calls=%async_computation.18 | async-start | bytes 13107200 | tf_op jit(solution)/shard_map/reduce_scatter | solution.py:248
  1849.6 106.0 %copy-start.7 = (bf16[1,16,64,1280]{3,2,1,0:T(8,128)(2,1)S(1)}, bf16[1,16,64,1280]{3,2,1,0:T(8,128)(2,1)}, u32[]{:S(2)}) copy-start(bf16[1,16,64,1280]{3,2,1,0:T(8,128)(2,1)} %param.17) | copy-start | bytes 7864324
  1849.6 106.0 %copy-start.33 = (f32[16,64]{1,0:T(8,128)S(1)}, f32[16,64]{1,0:T(8,128)}, u32[]{:S(2)}) copy-start(f32[16,64]{1,0:T(8,128)} %copy-done.32) | copy-start | bytes 12292
  1849.6 106.0 %copy-start.37 = (f32[1280]{0:T(1024)S(1)}, f32[1280]{0:T(1024)}, u32[]{:S(2)}) copy-start(f32[1280]{0:T(1024)} %copy-done.36) | copy-start | bytes 15364
  1852.4 107.0 %copy-start.47 = (f32[16,64]{1,0:T(8,128)S(1)}, f32[16,64]{1,0:T(8,128)}, u32[]{:S(2)}) copy-start(f32[16,64]{1,0:T(8,128)} %copy-done.46) | copy-start | bytes 12292
  1852.4 107.1 %copy-start.41 = (f32[16,64]{1,0:T(8,128)S(1)}, f32[16,64]{1,0:T(8,128)}, u32[]{:S(2)}) copy-start(f32[16,64]{1,0:T(8,128)} %copy-done.40) | copy-start | bytes 12292
  (91 other events, 484.1 us)
Sparse Core Ops, SparseCore 0:
  16.8 72.8 all-gather.7
  91.9 58.3 all-gather.9
  468.9 85.3 reduce-scatter.10
  556.3 61.9 all-gather.13
  620.3 68.7 all-gather.11
  691.2 61.9 all-gather.15
  773.4 83.8 reduce-scatter.12
  868.5 70.1 all-gather.17
  989.5 85.2 reduce-scatter.14
  1096.4 70.1 all-gather.19
  1170.2 76.0 reduce-scatter.22
  1250.2 74.9 reduce-scatter.20
  1731.5 63.6 reduce-scatter.18
  1798.9 69.6 reduce-scatter.24
  1871.2 84.3 reduce-scatter.16
where the time goes:
time: 2030 us; the launch traced here: 2020 us
  matrix products  677 us (33%)
  waiting for transfers between devices  575 us (28%)
  local copies, waits for them, and re-layouts  520 us (26%)
  blocking collectives  115 us (6%)
  other arithmetic  105 us (5%)
    reduce_scatter x1, waiting for transfers between devices, shards(): lax.psum_scatter(jnp.einsum('xym,dm->xyd', row_piece, up_matrix, preferre...  85.4 us
    reduce_scatter x1, waiting for transfers between devices, shards(): lax.psum_scatter(jnp.einsum('xyc,cd->xyd', row_piece, proj_full, preferre...  84.2 us
    reduce_scatter x1, waiting for transfers between devices, shards(): lax.psum_scatter(jnp.einsum('xym,md->xyd', row_piece, down_matrix, prefer...  84 us
    dot_general x10, matrix products, score_block(): jnp.einsum('wqhr,qkr->whqk', along_wide, wide_sel, precision=highest)  78 us
    dot_general x10, matrix products, score_block(): jnp.einsum('wqhr,qkr->whqk', along_high, high_sel, precision=highest)  77.8 us
    all_gather x1, waiting for transfers between devices, shards(): mlp_input = lax.all_gather(normed_two, 'tensor', axis=0, tiled=True)  70.8 us
    all_gather x1, waiting for transfers between devices, shards(): grad_rows = lax.all_gather(result_low, 'tensor', axis=0, tiled=True)  70.3 us
    dot_general x1, matrix products, shards(): jnp.einsum('xyd,dm->xym', mlp_input, up_matrix, preferred_element_type=jn...  60.9 us
  transfers between devices with their start and end apart: 15, of which 10 were waited for; matrix products, arithmetic and copies ran while one was open for 42% of the time, Pallas kernels for 0%

commit v1 on v0

--- a/solution.py
+++ b/solution.py
@@ -178,7 +178,14 @@
     ).astype(jnp.float32)
     middle = source + attn_branch + out_biases[0].astype(jnp.float32)
     normed_two = layer_norm(middle, gains_wide[1], shifts_wide[1]).astype(jnp.bfloat16)
-    mlp_input = lax.all_gather(normed_two, "tensor", axis=0, tiled=True)
+    arr_now, spare = (lax.psum(1, "tensor"), lax.axis_index("tensor"))
+    mlp_input, f_now = (normed_two, 1)
+    while f_now < arr_now:
+        state_now = lax.ppermute(mlp_input, "tensor", [(ix, ix ^ f_now) for ix in range(arr_now)])
+        carry = jnp.concatenate([mlp_input, state_now], axis=0)
+        carry_in = jnp.concatenate([state_now, mlp_input], axis=0)
+        mlp_input = jnp.where(spare & f_now == 0, carry, carry_in)
+        f_now = 2 * f_now
     hidden = (
         jnp.einsum("xyd,dm->xym", mlp_input, up_matrix, preferred_element_type=jnp.float32)
         + up_bias_all

time: 2030 us -> 2030 us (level)
    all_gather x1 -> x0, waiting for transfers between devices: 70.8 us -> none  [shards(): mlp_input = lax.all_gather(normed_two, 'tensor', axis=0, tiled=True)]
    ppermute x0 -> x2, waiting for transfers between devices: none -> 68.9 us  [shards(): lax.ppermute(mlp_input, 'tensor', [(ix, ix ^ f_now) for ix in range(arr_n...]
  transfers between devices with their start and end apart: 15 -> 16, of which waited for: 10 -> 10; matrix products, arithmetic and copies ran while one was open for 42% -> 42% of each run, Pallas kernels for 0% -> 0%
where the time goes in v1:
time: 2030 us; the launch traced here: 2020 us
  matrix products  685 us (34%)
  waiting for transfers between devices  564 us (28%)
  local copies, waits for them, and re-layouts  518 us (26%)
  blocking collectives  115 us (6%)
  other arithmetic  110 us (5%)
    reduce_scatter x1, waiting for transfers between devices, shards(): lax.psum_scatter(jnp.einsum('xym,md->xyd', row_piece, down_matrix, prefer...  85.4 us
    reduce_scatter x1, waiting for transfers between devices, shards(): lax.psum_scatter(jnp.einsum('xym,dm->xyd', row_piece, up_matrix, preferre...  85.4 us
    reduce_scatter x1, waiting for transfers between devices, shards(): lax.psum_scatter(jnp.einsum('xyc,cd->xyd', row_piece, proj_full, preferre...  84.2 us
    dot_general x10, matrix products, score_block(): jnp.einsum('wqhr,qkr->whqk', along_high, high_sel, precision=highest)  77.4 us
    dot_general x10, matrix products, score_block(): jnp.einsum('wqhr,qkr->whqk', along_wide, wide_sel, precision=highest)  77.3 us
    all_gather x1, waiting for transfers between devices, shards(): grad_rows = lax.all_gather(result_low, 'tensor', axis=0, tiled=True)  70.3 us
    ppermute x2, waiting for transfers between devices, shards(): lax.ppermute(mlp_input, 'tensor', [(ix, ix ^ f_now) for ix in range(arr_n...  68.9 us
    dot_general x1, matrix products, shards(): jnp.einsum('xyd,dm->xym', mlp_input, up_matrix, preferred_element_type=jn...  68.6 us
  transfers between devices with their start and end apart: 16, of which 10 were waited for; matrix products, arithmetic and copies ran while one was open for 42% of the time, Pallas kernels for 0%

profile of v1, /device:TPU:0, one launch (start us, length us, event | category | flops | bytes accessed | tf_op | source)
XLA Modules:
  0.0 2020.8 jit_solution(8673895277755603607)
XLA Ops:
  18.5 36.7 %all_gather.23 = bf16[320,1280]{0,1:T(8,128)(2,1)} all-gather(bf16[320,160]{0,1:T(8,128)(2,1)S(1)} %copy-done.44), channel_id=1, replica_groups=mesh['dp'=8,'tensor'=4] {'dp'}, dimensions={1}, use_global_device_ids=true | all-gather | bytes 921600 | tf_op jit(solution)/shard_map/all_gather | solution.py:145
  55.2 34.5 %all-gather.7.cloned.1.call-done = bf16[64,64,1280]{2,1,0:T(8,128)(2,1)} async-done(((bf16[16,64,1280]{2,1,0:T(8,128)(2,1)}), bf16[64,64,1280]{2,1,0:T(8,128)(2,1)}) %all-gather.7.cloned.1.call-update) | async-done | bytes 10485776 | tf_op jit(solution)/shard_map/all_gather | solution.py:160
  99.9 18.6 reshape.295
  118.6 13.4 copy.189
  131.9 19.4 reshape.319
  151.4 24.6 %fusion.109 = f32[3,5,5,196,320]{4,3,0,2,1:T(8,128)} fusion(bf16[5,5,196,1280,1]{3,2,1,0,4:T(8,128)(2,1)} %reshape.319, bf16[3,1280,320]{2,1,0:T(8,128)(2,1)} %all-gather.9.cloned.1.call-done), kind=kOutput, calls=%fused_computation.143 | convolution fusion | flops 12042240000 | bytes 33817600 | tf_op jit(solution)/shard_map/abpd,sdc->sabpc/dot_general | solution.py:162
  176.0 11.8 fusion.167
  231.4 193.3 %while.31 = (s32[]{:T(128)}, bf16[5,5,196,4,80]{2,4,3,1,0:T(8,128)(2,1)}, f32[5,5,4,196]{3,2,1,0:T(4,128)}, bf16[5,5,196,4,80]{2,4,3,1,0:T(8,128)(2,1)}, bf16[5,...) while((s32[]{:T(128)}, ...), condition=%wide.region_5.6_spmd.clone, body=%wide.region_2.5_spmd.clone.sunk | while | flops 322814336 | bytes 44160668 | solution.py:166
  424.7 11.4 copy.121
  470.4 84.2 %reduce-scatter.11.cloned.1.call-done = bf16[16,64,1280]{2,1,0:T(8,128)(2,1)} async-done(((bf16[64,64,1280]{2,1,0:T(8,128)(2,1)}), bf16[16,64,1280]{2,1,0:T(8,128)(2,1)}) %reduce-scatter.11.cloned.1.call-update) | async-done | bytes 2621456 | tf_op jit(solution)/shard_map/reduce_scatter | solution.py:171
  572.6 51.1 %all-gather.11.cloned.1.call-done = bf16[1280,1280]{1,0:T(8,128)(2,1)} async-done(((bf16[160,1280]{1,0:T(8,128)(2,1)}), bf16[1280,1280]{1,0:T(8,128)(2,1)}) %all-gather.11.cloned.1.call-update) | async-done | bytes 3276816 | tf_op jit(solution)/shard_map/all_gather | solution.py:146
  623.7 63.9 %collective-permute-done.1 = bf16[32,64,1280]{2,1,0:T(8,128)(2,1)} collective-permute-done((bf16[32,64,1280]{2,1,0:T(8,128)(2,1)}, bf16[32,64,1280]{2,1,0:T(8,128)(2,1)}, u32[]{:S(2)}, u32[]{:S(2)}) %collective-permute-start.1) | collective-permute-done | bytes 5242912 | tf_op jit(solution)/shard_map/ppermute | solution.py:184
  687.6 68.6 %multiply_convert_fusion = (bf16[64,64,1280]{2,1,0:T(8,128)(2,1)}, f32[64,64,1280]{2,1,0:T(8,128)}, f32[64,64,1280]{2,1,0:T(8,128)}) fusion(f32[1280]{0:T(1024)S(1)} %convert_element_type.209, bf16[1280,1280]{1,0:T(8,128)(2,1)} %all-gather.11.cloned.1.call-done, bf16[32,64,1280]{2,1,0:T(8,128)(2,1)} %collective-permute-done.1, ...), kind=kOutput, calls=%fused_computation.117 | convolution fusion | flops 13783531520 | bytes 66196480 | tf_op jit(solution)/shard_map/xyd,dm->xym/dot_general | solution.py:190
  756.2 20.2 %convolution_convert_fusion.1 = bf16[64,64,1280]{2,1,0:T(8,128)(2,1)} fusion(bf16[64,64,1280]{2,1,0:T(8,128)(2,1)} %get-tuple-element.415, bf16[1280,1280]{0,1:T(8,128)(2,1)} %all-gather.13.cloned.1.call-done), kind=kOutput, calls=%fused_computation.135 | convolution fusion | flops 13427015680 | bytes 24248320 | tf_op jit(solution)/shard_map/xym,md->xyd/dot_general | solution.py:196
  776.5 85.4 %reduce-scatter.13.cloned.1.call-done = bf16[16,64,1280]{2,1,0:T(8,128)(2,1)} async-done(((bf16[64,64,1280]{2,1,0:T(8,128)(2,1)}), bf16[16,64,1280]{2,1,0:T(8,128)(2,1)}) %reduce-scatter.13.cloned.1.call-update) | async-done | bytes 2621456 | tf_op jit(solution)/shard_map/reduce_scatter | solution.py:195
  872.9 70.3 %all-gather.15.cloned.1.call-done = bf16[64,64,1280]{2,1,0:T(8,128)(2,1)} async-done(((bf16[16,64,1280]{2,1,0:T(8,128)(2,1)}), bf16[64,64,1280]{2,1,0:T(8,128)(2,1)}) %all-gather.15.cloned.1.call-update) | async-done | bytes 10485776 | tf_op jit(solution)/shard_map/all_gather | solution.py:209
  943.2 30.5 %fusion.171 = (f32[1280]{0:T(1024)}, bf16[64,64,1280]{2,1,0:T(8,128)(2,1)}) fusion(f32[64,64,1280]{2,1,0:T(8,128)} %get-tuple-element.416, f32[64,64,1280]{2,1,0:T(8,128)} %get-tuple-element.430, bf16[64,64,1280]{2,1,0:T(8,128)(2,1)} %all-gather.15.cloned.1.call-done, bf16[1280,1280]{0,1:T(8,128)(2,1)} %all-gather.13.cloned.1.call-done), kind=kOutput, calls=%fused_computation.256 | convolution fusion | flops 13500414976 | bytes 66196480 | tf_op jit(solution)/shard_map/xyd,md->xym/dot_general | solution.py:211
  973.7 19.8 convolution_convert_fusion
  993.6 85.4 %reduce-scatter.15.cloned.1.call-done = bf16[16,64,1280]{2,1,0:T(8,128)(2,1)} async-done(((bf16[64,64,1280]{2,1,0:T(8,128)(2,1)}), bf16[16,64,1280]{2,1,0:T(8,128)(2,1)}) %reduce-scatter.15.cloned.1.call-update) | async-done | bytes 2621456 | tf_op jit(solution)/shard_map/reduce_scatter | solution.py:220
  1100.7 20.8 %fusion.112 = bf16[1280,1280]{0,1:T(8,128)(2,1)} fusion(bf16[64,64,1280]{2,1,0:T(8,128)(2,1)} %get-tuple-element.415, bf16[64,64,1280]{2,1,0:T(8,128)(2,1)} %all-gather.15.cloned.1.call-done), kind=kOutput, calls=%fused_computation.157 | convolution fusion | flops 13423411200 | bytes 24248320 | tf_op jit(solution)/shard_map/xym,xyd->md/dot_general | solution.py:210
  1121.6 23.0 %fusion.113 = bf16[1280,1280]{1,0:T(8,128)(2,1)} fusion(bf16[64,64,1280]{2,1,0:T(8,128)(2,1)} %get-tuple-element.432, bf16[32,64,1280]{2,1,0:T(8,128)(2,1)} %collective-permute-done.1, bf16[32,64,1280]{2,1,0:T(8,128)(2,1)} %maximum_select_fusion.1, pred[]{:T(512)S(6)} %eq.64), kind=kOutput, calls=%fused_computation.158 | convolution fusion | flops 13439139840 | bytes 24248320 | tf_op jit(solution)/shard_map/xyd,xym->dm/dot_general | solution.py:218
  1144.7 26.3 %all-gather.17.cloned.1.call-done = bf16[64,64,1280]{2,1,0:T(8,128)(2,1)} async-done(((bf16[16,64,1280]{2,1,0:T(8,128)(2,1)}), bf16[64,64,1280]{2,1,0:T(8,128)(2,1)}) %all-gather.17.cloned.1.call-update) | async-done | bytes 10485776 | tf_op jit(solution)/shard_map/all_gather | solution.py:233
  1204.3 11.4 copy.124
  1215.7 466.2 %while.32 = (s32[]{:T(128)}, f32[5,5,196,4,80]{2,4,3,1,0:T(8,128)}, bf16[5,5,196,4,80]{2,4,3,1,0:T(8,128)(2,1)}, f32[5,5,196,4,80]{2,4,3,1,0:T(8,128)}, f32[5,2,...) while((s32[]{:T(128)}, f32[5,5,196,4,80]{2,4,3,1,0:T(8,128)}, ...), condition=%wide.region_17.18_spmd.clone.clone, body=%wide.region_13.17_spmd.clone.clone.sunk | while | flops 1137800704 | bytes 142737584 | solution.py:241
  1733.8 17.5 fusion.143
  1765.6 25.6 %bitcast_convert_fusion = bf16[5,5,196,1280]{3,2,1,0:T(8,128)(2,1)} fusion(bf16[1,5,5,196,320]{4,3,0,2,1:T(8,128)(2,1)} %copy.127, bf16[1,5,5,196,320]{4,3,0,2,1:T(8,128)(2,1)} %copy.126, bf16[1,5,5,196,320]{4,3,0,2,1:T(8,128)(2,1)} %copy.125, bf16[3,1280,320]{2,1,0:T(8,128)(2,1)} %all-gather.9.cloned.1.call-done), kind=kOutput, calls=%fused_computation.114 | convolution fusion | flops 12057920512 | bytes 24409600 | tf_op jit(solution)/shard_map/sabpc,sdc->abpd/dot_general | solution.py:252
  1791.2 19.4 reshape.299
  1810.6 13.0 copy.188
  1823.6 18.7 reshape.300
  1856.7 37.6 %all-reduce.3 = (f32[2,320]{1,0:T(2,128)}, f32[1280]{0:T(1024)}) all-reduce(f32[2,320]{1,0:T(2,128)S(1)} %pad_maximum_fusion.10, f32[1280]{0:T(1024)S(1)} %copy-done.57), channel_id=1, replica_groups=mesh['dp'=8,'tensor'=4] {'dp'}, use_global_device_ids=true, to_apply=%region_29.30 | all-reduce | flops 1920 | bytes 15360 | tf_op jit(solution)/shard_map/psum | solution.py:277
  1900.7 57.2 %reduce-scatter.17.cloned.1.call-done = bf16[16,64,1280]{2,1,0:T(8,128)(2,1)} async-done(((bf16[64,64,1280]{2,1,0:T(8,128)(2,1)}), bf16[16,64,1280]{2,1,0:T(8,128)(2,1)}) %reduce-scatter.17.cloned.1.call-update) | async-done | bytes 2621456 | tf_op jit(solution)/shard_map/reduce_scatter | solution.py:255
  1964.9 41.0 %all-reduce.2 = (f32[]{:T(128)}, f32[2,1280]{1,0:T(2,128)}, f32[2,1280]{1,0:T(2,128)}, f32[2,1280]{1,0:T(2,128)}, f32[2,27,80]{2,1,0:T(8,128)S(1)}) all-reduce(f32[]{:T(128)} %get-tuple-element.343, f32[2,1280]{1,0:T(2,128)S(1)} %pad_maximum_fusion.7, ...), channel_id=1, replica_groups=mesh['dp'=8,'tensor'=4] {'dp','tensor'}, use_global_device_ids=true, to_apply=%region_22.23 | all-reduce | flops 12001 | bytes 96008 | tf_op jit(solution)/shard_map/psum | solution.py:278
  (557 shorter events, 932.2 us)
Async XLA Ops:
  7.2 82.5 %all-gather.7.cloned.1.call-start = ((), (), s32[]{:S(2)}) async-start(), calls=%async_computation.8 | async-start | bytes 13107200 | tf_op jit(solution)/shard_map/all_gather | solution.py:160
  16.6 134.7 %all-gather.9.cloned.1.call-start = ((), (), s32[]{:S(2)}) async-start(), calls=%async_computation.9 | async-start | bytes 3317760 | tf_op jit(solution)/shard_map/all_gather | solution.py:144
  17.4 537.2 %reduce-scatter.11.cloned.1.call-start = ((), (), s32[]{:S(2)}) async-start(), calls=%async_computation.10 | async-start | bytes 13107200 | tf_op jit(solution)/shard_map/reduce_scatter | solution.py:171
  424.7 21.5 %copy-start.18 = (s32[196,14]{1,0:T(8,128)}, s32[196,14]{1,0:T(8,128)S(1)}, u32[]{:S(2)}) copy-start(s32[196,14]{1,0:T(8,128)S(1)} %get-tuple-element.696) | copy-start | bytes 32932
  469.1 85.5 %copy-start.5 = (bf16[1,16,64,1280]{3,2,1,0:T(8,128)(2,1)S(1)}, bf16[1,16,64,1280]{3,2,1,0:T(8,128)(2,1)}, u32[]{:S(2)}) copy-start(bf16[1,16,64,1280]{3,2,1,0:T(8,128)(2,1)} %param.17) | copy-start | bytes 7864324
  469.1 154.7 %all-gather.11.cloned.1.call-start = ((), (), s32[]{:S(2)}) async-start(), calls=%async_computation.11 | async-start | bytes 3686400 | tf_op jit(solution)/shard_map/all_gather | solution.py:146
  470.4 88.4 %copy-start.30 = (f32[1280]{0:T(1024)}, f32[1280]{0:T(1024)S(1)}, u32[]{:S(2)}) copy-start(f32[1280]{0:T(1024)S(1)} %get-tuple-element.352) | copy-start | bytes 15364
  561.4 5.2 collective-permute-start
  561.5 194.7 %all-gather.13.cloned.1.call-start = ((), (), s32[]{:S(2)}) async-start(), calls=%async_computation.12 | async-start | bytes 3686400 | tf_op jit(solution)/shard_map/all_gather | solution.py:147
  572.2 115.4 %collective-permute-start.1 = (bf16[32,64,1280]{2,1,0:T(8,128)(2,1)}, bf16[32,64,1280]{2,1,0:T(8,128)(2,1)}, u32[]{:S(2)}, u32[]{:S(2)}) collective-permute-start(bf16[32,64,1280]{2,1,0:T(8,128)(2,1)} %maximum_select_fusion.1), channel_id=1, source_target_pairs={{0,2},{1,3},{2,0},{3,1},{4,6},{5,7},{6,4},{7,5},{8,10},{9,11},{10,... | collective-permute-start | bytes 15728648 | tf_op jit(solution)/shard_map/ppermute | solution.py:184
  572.5 289.4 %reduce-scatter.13.cloned.1.call-start = ((), (), s32[]{:S(2)}) async-start(), calls=%async_computation.13 | async-start | bytes 13107200 | tf_op jit(solution)/shard_map/reduce_scatter | solution.py:195
  776.4 85.5 %copy-start.6 = (bf16[1,16,64,1280]{3,2,1,0:T(8,128)(2,1)S(1)}, bf16[1,16,64,1280]{3,2,1,0:T(8,128)(2,1)}, u32[]{:S(2)}) copy-start(bf16[1,16,64,1280]{3,2,1,0:T(8,128)(2,1)} %param.17) | copy-start | bytes 7864324
  776.4 85.5 %copy-start.31 = (f32[1280]{0:T(1024)S(1)}, f32[1280]{0:T(1024)}, u32[]{:S(2)}) copy-start(f32[1280]{0:T(1024)} %copy-done.30) | copy-start | bytes 15364
  776.4 85.5 %copy-start.45 = (f32[1280]{0:T(1024)S(1)}, f32[1280]{0:T(1024)}, u32[]{:S(2)}) copy-start(f32[1280]{0:T(1024)} %get-tuple-element.353) | copy-start | bytes 15364
  776.5 166.8 %all-gather.15.cloned.1.call-start = ((), (), s32[]{:S(2)}) async-start(), calls=%async_computation.14 | async-start | bytes 13107200 | tf_op jit(solution)/shard_map/all_gather | solution.py:209
  872.9 206.2 %reduce-scatter.15.cloned.1.call-start = ((), (), s32[]{:S(2)}) async-start(), calls=%async_computation.15 | async-start | bytes 13107200 | tf_op jit(solution)/shard_map/reduce_scatter | solution.py:220
  993.5 85.5 %copy-start.35 = (f32[16,64]{1,0:T(8,128)S(1)}, f32[16,64]{1,0:T(8,128)}, u32[]{:S(2)}) copy-start(f32[16,64]{1,0:T(8,128)} %copy-done.34) | copy-start | bytes 12292
  993.5 85.5 %copy-start.39 = (f32[1280]{0:T(1024)S(1)}, f32[1280]{0:T(1024)}, u32[]{:S(2)}) copy-start(f32[1280]{0:T(1024)} %get-tuple-element.349) | copy-start | bytes 15364
  993.6 90.9 %copy-start.49 = (f32[16,64]{1,0:T(8,128)S(1)}, f32[16,64]{1,0:T(8,128)}, u32[]{:S(2)}) copy-start(f32[16,64]{1,0:T(8,128)} %copy-done.48) | copy-start | bytes 12292
  993.6 90.9 %copy-start.43 = (f32[16,64]{1,0:T(8,128)S(1)}, f32[16,64]{1,0:T(8,128)}, u32[]{:S(2)}) copy-start(f32[16,64]{1,0:T(8,128)} %copy-done.42) | copy-start | bytes 12292
  993.6 177.4 %all-gather.17.cloned.1.call-start = ((), (), s32[]{:S(2)}) async-start(), calls=%async_computation.16 | async-start | bytes 13107200 | tf_op jit(solution)/shard_map/all_gather | solution.py:233
  1100.6 751.7 %reduce-scatter.23.cloned.1.call-start = ((), (), s32[]{:S(2)}) async-start(), calls=%async_computation.20 | async-start | bytes 3686400 | tf_op jit(solution)/shard_map/reduce_scatter | solution.py:273
  1121.5 732.9 %reduce-scatter.21.cloned.1.call-start = ((), (), s32[]{:S(2)}) async-start(), calls=%async_computation.19 | async-start | bytes 3686400 | tf_op jit(solution)/shard_map/reduce_scatter | solution.py:270
  1121.6 49.4 %copy-start.29 = (bf16[320,1280]{0,1:T(8,128)(2,1)S(1)}, bf16[320,1280]{0,1:T(8,128)(2,1)}, u32[]{:S(2)}) copy-start(bf16[320,1280]{0,1:T(8,128)(2,1)} %all_gather.23) | copy-start | bytes 2457604
  1144.6 749.7 %reduce-scatter.19.cloned.1.call-start = ((), (), s32[]{:S(2)}) async-start(), calls=%async_computation.18 | async-start | bytes 1105920 | tf_op jit(solution)/shard_map/reduce_scatter | solution.py:267
  1733.7 162.2 %reduce-scatter.25.cloned.1.call-start = ((), (), s32[]{:S(2)}) async-start(), calls=%async_computation.21 | async-start | bytes 2949120
  1765.6 192.4 %reduce-scatter.17.cloned.1.call-start = ((), (), s32[]{:S(2)}) async-start(), calls=%async_computation.17 | async-start | bytes 13107200 | tf_op jit(solution)/shard_map/reduce_scatter | solution.py:255
  1851.6 106.3 %copy-start.7 = (bf16[1,16,64,1280]{3,2,1,0:T(8,128)(2,1)S(1)}, bf16[1,16,64,1280]{3,2,1,0:T(8,128)(2,1)}, u32[]{:S(2)}) copy-start(bf16[1,16,64,1280]{3,2,1,0:T(8,128)(2,1)} %param.17) | copy-start | bytes 7864324
  1851.6 106.3 %copy-start.33 = (f32[16,64]{1,0:T(8,128)S(1)}, f32[16,64]{1,0:T(8,128)}, u32[]{:S(2)}) copy-start(f32[16,64]{1,0:T(8,128)} %copy-done.32) | copy-start | bytes 12292
  1851.7 106.3 %copy-start.37 = (f32[1280]{0:T(1024)S(1)}, f32[1280]{0:T(1024)}, u32[]{:S(2)}) copy-start(f32[1280]{0:T(1024)} %copy-done.36) | copy-start | bytes 15364
  1854.4 107.4 %copy-start.47 = (f32[16,64]{1,0:T(8,128)S(1)}, f32[16,64]{1,0:T(8,128)}, u32[]{:S(2)}) copy-start(f32[16,64]{1,0:T(8,128)} %copy-done.46) | copy-start | bytes 12292
  1854.4 107.4 %copy-start.41 = (f32[16,64]{1,0:T(8,128)S(1)}, f32[16,64]{1,0:T(8,128)}, u32[]{:S(2)}) copy-start(f32[16,64]{1,0:T(8,128)} %copy-done.40) | copy-start | bytes 12292
  (92 other events, 516.7 us)
Sparse Core Ops, SparseCore 0:
  16.8 72.8 all-gather.6
  91.9 58.3 all-gather.8
  469.2 85.3 reduce-scatter.10
  561.6 62.0 all-gather.10
  625.8 60.5 all-gather.12
  776.6 85.3 reduce-scatter.12
  873.0 70.1 all-gather.14
  993.7 85.2 reduce-scatter.14
  1100.7 70.1 all-gather.16
  1174.4 76.0 reduce-scatter.22
  1254.6 75.0 reduce-scatter.20
  1733.8 63.6 reduce-scatter.18
  1801.4 69.5 reduce-scatter.24
  1873.7 84.2 reduce-scatter.16
